TPU v7x, 32 devices: a whole 2x2x4 slice. The times are simulated.
32 devices in a mesh: depth: 4 (over z), tile: 8 (over y, x, core).
Axes of the slice: x: 2, y: 2, z: 4, core: 2. Of those that a mesh axis runs over, the one named last changes fastest.
Arguments:
- transmission: bfloat16 [2, 8, 2048, 2048], P(None, 'depth', 'tile')
- probe: float32 [2, 128, 128], replicated, may hold values from -6 to 6
- propagator: float32 [128, 128], replicated, may hold values from -3.140625 to 3.140625
- measured: float32 [64, 128, 128], P('tile'), may hold values from 0.2 to 3
- positions: int32 [64, 2], P('tile'), may hold values from 0 to 1920, as said below
- counts: int32 [8], P('tile'), may hold values from 1 to 8, as said below
Outputs:
- object_grad: float32 [2, 8, 2048, 2048], P(None, 'depth', 'tile')
Inputs may be any that keep to these rules, and one draw needn't show every extreme that they name: `positions`: A window's first row lies from 0 to 256 in the strip's rows extended by 64 above, its first column from 0 to 1920; both ends of both ranges occur in every draw. `counts`: some strip has all 8 slots live and some strip only one.
All inputs are finite; a program needn't handle non-finite values.
Results may differ from a plain program's by a relative error of at most 0.0003.
Values may be sent and summed in bfloat16 or wider, within the bound.
No kernel may reach another device: no remote copies, remote signals or barrier semaphores. Data moves between devices by JAX's collectives and lax.ppermute only.
A program may use at most 128 MiB of HBM per device.

v0:
```python
import math

import jax
import jax.numpy as jnp
from jax import lax
from jax.sharding import PartitionSpec as P

DELTA = 0.1
HIGHEST = lax.Precision.HIGHEST


def with_halo(block, sides, width):
    for axis, dim in sides:
        count = lax.axis_size(axis)
        forward = [(i, i + 1) for i in range(count - 1)]
        forward.append((count - 1, 0))
        backward = [(target, source) for source, target in forward]
        low = lax.ppermute(
            lax.slice_in_dim(block, block.shape[dim] - width, None, axis=dim), axis, forward
        )
        high = lax.ppermute(lax.slice_in_dim(block, 0, width, axis=dim), axis, backward)
        block = jnp.concatenate([low, block, high], axis=dim)
    return block


def passed_along(array, axis, by):
    length = lax.axis_size(axis)
    pairs = [(i, i + by) for i in range(length) if 0 <= i + by < length]
    return lax.ppermute(array, axis, pairs)


def tables(width):
    index = jnp.arange(width, dtype=jnp.int32)
    product = index[:, None] * index[None, :] % width
    angle = product.astype(jnp.float32) * (2.0 * math.pi / width)
    scale = 1.0 / math.sqrt(width)
    return (jnp.cos(angle) * scale, jnp.sin(angle) * scale)


def transform(wave_real, wave_imag, cos_table, sin_table, sign):
    sin_signed = sign * sin_table
    mid_real = jnp.einsum("jk,bkl->bjl", cos_table, wave_real, precision=HIGHEST) - jnp.einsum(
        "jk,bkl->bjl", sin_signed, wave_imag, precision=HIGHEST
    )
    mid_imag = jnp.einsum("jk,bkl->bjl", cos_table, wave_imag, precision=HIGHEST) + jnp.einsum(
        "jk,bkl->bjl", sin_signed, wave_real, precision=HIGHEST
    )
    out_real = jnp.einsum("bjk,kl->bjl", mid_real, cos_table, precision=HIGHEST) - jnp.einsum(
        "bjk,kl->bjl", mid_imag, sin_signed, precision=HIGHEST
    )
    out_imag = jnp.einsum("bjk,kl->bjl", mid_imag, cos_table, precision=HIGHEST) + jnp.einsum(
        "bjk,kl->bjl", mid_real, sin_signed, precision=HIGHEST
    )
    return (out_real, out_imag)


def propagate(wave_real, wave_imag, kernel_real, kernel_imag, cos_table, sin_table):
    freq_real, freq_imag = transform(wave_real, wave_imag, cos_table, sin_table, -1.0)
    prod_real = freq_real * kernel_real - freq_imag * kernel_imag
    prod_imag = freq_real * kernel_imag + freq_imag * kernel_real
    return transform(prod_real, prod_imag, cos_table, sin_table, 1.0)


def forward_slices(wave, windows, kernel_real, kernel_imag, cos_table, sin_table):
    wave_real, wave_imag = (wave[:, 0], wave[:, 1])
    stored = []
    levels = windows.shape[2]
    phi_real, phi_imag = (wave_real, wave_imag)
    for level in range(levels):
        stored.append(jnp.stack([wave_real, wave_imag], 1))
        trans_real = windows[:, 0, level].astype(jnp.float32)
        trans_imag = windows[:, 1, level].astype(jnp.float32)
        phi_real = wave_real * trans_real - wave_imag * trans_imag
        phi_imag = wave_real * trans_imag + wave_imag * trans_real
        wave_real, wave_imag = propagate(
            phi_real, phi_imag, kernel_real, kernel_imag, cos_table, sin_table
        )
    outgoing = jnp.stack([wave_real, wave_imag], 1)
    return (jnp.stack(stored, 2), jnp.stack([phi_real, phi_imag], 1), outgoing)


def backward_slices(grad, stored, windows, kernel_real, kernel_imag, cos_table, sin_table):
    grad_real, grad_imag = (grad[:, 0], grad[:, 1])
    levels = windows.shape[2]
    pieces = [None] * levels
    for level in reversed(range(levels)):
        wave_real = stored[:, 0, level]
        wave_imag = stored[:, 1, level]
        trans_real = windows[:, 0, level].astype(jnp.float32)
        trans_imag = windows[:, 1, level].astype(jnp.float32)
        piece_real = wave_real * grad_real + wave_imag * grad_imag
        piece_imag = wave_real * grad_imag - wave_imag * grad_real
        pieces[level] = jnp.stack([piece_real, piece_imag], 1)
        back_real = trans_real * grad_real + trans_imag * grad_imag
        back_imag = trans_real * grad_imag - trans_imag * grad_real
        grad_real, grad_imag = propagate(
            back_real, back_imag, kernel_real, -kernel_imag, cos_table, sin_table
        )
    return (jnp.stack(pieces, 2), jnp.stack([grad_real, grad_imag], 1))


def far_field(exit_wave, amplitude, live, cos_table, sin_table):
    freq_real, freq_imag = transform(exit_wave[:, 0], exit_wave[:, 1], cos_table, sin_table, -1.0)
    modulus = jnp.sqrt(freq_real * freq_real + freq_imag * freq_imag + DELTA)
    weight = live[:, None, None] * (modulus - amplitude) / modulus
    back_real, back_imag = transform(
        weight * freq_real, weight * freq_imag, cos_table, sin_table, 1.0
    )
    return jnp.stack([back_real, back_imag], 1)


def body(transmission, probe, propagator, measured, positions, counts):
    width = probe.shape[1]
    halo_rows = width // 2
    levels = transmission.shape[1]
    tile_rows = transmission.shape[2]
    columns = transmission.shape[3]
    slots = positions.shape[0]
    cos_table, sin_table = tables(width)
    kernel_real = jnp.cos(propagator)
    kernel_imag = jnp.sin(propagator)
    live = (jnp.arange(slots, dtype=jnp.int32) < counts[0]).astype(jnp.float32)
    depth_count = lax.axis_size("depth")
    depth_index = lax.axis_index("depth")
    padded = with_halo(transmission, (("tile", 2),), halo_rows)

    def window_at(corner):
        return lax.dynamic_slice(padded, (0, 0, corner[0], corner[1]), (2, levels, width, width))

    windows = jax.vmap(window_at)(positions)
    groups = 2
    batch = slots // groups
    sections = depth_count + groups - 1
    probe_batch = jnp.broadcast_to(probe[None], (batch, 2, width, width))
    stored_all = jnp.zeros((slots, 2, levels, width, width), jnp.float32)
    exits = jnp.zeros((slots, 2, width, width), jnp.float32)
    received = jnp.zeros((batch, 2, width, width), jnp.float32)
    for section in range(sections):
        group = section - depth_index
        active = (group >= 0) & (group < groups)
        start = jnp.clip(group, 0, groups - 1) * batch
        wave_in = jnp.where(depth_index == 0, probe_batch, received)
        group_windows = lax.dynamic_slice_in_dim(windows, start, batch, 0)
        stored, last_phi, outgoing = forward_slices(
            wave_in, group_windows, kernel_real, kernel_imag, cos_table, sin_table
        )
        old_stored = lax.dynamic_slice_in_dim(stored_all, start, batch, 0)
        stored_all = lax.dynamic_update_slice_in_dim(
            stored_all, jnp.where(active, stored, old_stored), start, 0
        )
        old_exits = lax.dynamic_slice_in_dim(exits, start, batch, 0)
        exits = lax.dynamic_update_slice_in_dim(
            exits, jnp.where(active, last_phi, old_exits), start, 0
        )
        if section + 1 < sections:
            received = passed_along(outgoing, "depth", 1)
    far_grads = far_field(exits, measured, live, cos_table, sin_table)
    grad_windows = jnp.zeros((slots, 2, levels, width, width), jnp.float32)
    received = jnp.zeros((batch, 2, width, width), jnp.float32)
    for section in range(sections):
        group = section - (depth_count - 1 - depth_index)
        active = (group >= 0) & (group < groups)
        start = jnp.clip(group, 0, groups - 1) * batch
        grad_in = jnp.where(
            depth_index == depth_count - 1,
            lax.dynamic_slice_in_dim(far_grads, start, batch, 0),
            received,
        )
        group_windows = lax.dynamic_slice_in_dim(windows, start, batch, 0)
        stored = lax.dynamic_slice_in_dim(stored_all, start, batch, 0)
        pieces, outgoing = backward_slices(
            grad_in, stored, group_windows, kernel_real, kernel_imag, cos_table, sin_table
        )
        old_pieces = lax.dynamic_slice_in_dim(grad_windows, start, batch, 0)
        grad_windows = lax.dynamic_update_slice_in_dim(
            grad_windows, jnp.where(active, pieces, old_pieces), start, 0
        )
        if section + 1 < sections:
            received = passed_along(outgoing, "depth", -1)

    def add_window(index, total):
        corner = positions[index]
        current = lax.dynamic_slice(total, (0, 0, corner[0], corner[1]), (2, levels, width, width))
        return lax.dynamic_update_slice(
            total, current + grad_windows[index], (0, 0, corner[0], corner[1])
        )

    grad_strip = jnp.zeros((2, levels, tile_rows + 2 * halo_rows, columns), jnp.float32)
    grad_strip = lax.fori_loop(0, slots, add_window, grad_strip)
    upper = grad_strip[:, :, :halo_rows]
    lower = grad_strip[:, :, tile_rows + halo_rows :]
    both_rims = jnp.concatenate([upper, lower], 2)
    framed = with_halo(both_rims, (("tile", 2),), halo_rows)
    center = grad_strip[:, :, halo_rows : halo_rows + tile_rows]
    center = center.at[:, :, :halo_rows].add(framed[:, :, :halo_rows])
    center = center.at[:, :, tile_rows - halo_rows :].add(framed[:, :, 3 * halo_rows :])
    return center


def solution(mesh):
    in_specs = (
        P(None, "depth", "tile", None),
        P(),
        P(),
        P("tile", None, None),
        P("tile", None),
        P("tile"),
    )
    out_specs = P(None, "depth", "tile", None)
    return jax.shard_map(body, mesh=mesh, in_specs=in_specs, out_specs=out_specs, check_vma=False)
```

profile of v0, /device:TPU:0, one launch (start us, length us, event | category | flops | bytes accessed | tf_op | source)
XLA Modules:
  0.0 568.0 jit_solution(1719434153587452023)
XLA Ops:
  7.0 20.9 %collective-permute-done = bf16[2,2,64,2048]{3,2,1,0:T(8,128)(2,1)S(1)} collective-permute-done((bf16[2,2,64,2048]{3,2,1,0:T(8,128)(2,1)}, bf16[2,2,64,2048]{3,2,1,0:T(8,128)(2,1)S(1)}, u32[]{:S(2)}, u32[]{:S(2)}) %collective-permute-start) | collective-permute-done | bytes 1048608 | tf_op jit(solution)/shard_map/ppermute | solution.py:18
  29.5 7.6 %pad_maximum_fusion = bf16[2,2,384,2048]{3,2,1,0:T(8,128)(2,1)} fusion(bf16[2,2,64,2048]{3,2,1,0:T(8,128)(2,1)} %collective-permute-done.1, bf16[2,2,256,2048]{3,2,1,0:T(8,128)(2,1)} %param.12, bf16[2,2,64,2048]{3,2,1,0:T(8,128)(2,1)S(1)} %collective-permute-done), kind=kLoop, calls=%fused_computation.6 | loop fusion | flops 18874368 | bytes 12582912 | tf_op jit(solution)/shard_map/concatenate | solution.py:22
  37.1 24.8 %while.17 = (s32[]{:T(128)}, bf16[2,2,384,2048]{3,2,1,0:T(8,128)(2,1)}, s32[8,4]{0,1:T(4,128)S(1)}, bf16[8,2,2,128,128]{4,3,0,2,1:T(8,128)(2,1)S(1)}, s32[]{:T(128)}) while((s32[]{:T(128)}, bf16[2,2,384,2048]{3,2,1,0:T(8,128)(2,1)}, s32[8,4]{0,1:T(4,128)S(1)}, bf16[8,2,2,128,128]{4,3,0,2,1:T(8,128)(2,1)S(1)}, s32[]{:T(128)}) %tuple.111), condition=%wide.while_cond.2, body=%wide.while_body.2.sunk | while | flops 2 | bytes 262277 | solution.py:128
  90.7 11.5 %collective-permute-done.2 = f32[4,2,128,128]{3,2,0,1:T(8,128)S(1)} collective-permute-done((f32[4,2,128,128]{3,2,0,1:T(8,128)S(1)}, f32[4,2,128,128]{3,2,0,1:T(8,128)S(1)}, u32[]{:S(2)}, u32[]{:S(2)}) %collective-permute-start.2) | collective-permute-done | bytes 524320 | tf_op jit(solution)/shard_map/ppermute | solution.py:29
  129.1 4.4 collective-permute-start.3
  133.5 12.2 %collective-permute-done.3 = f32[4,2,128,128]{3,2,0,1:T(8,128)S(1)} collective-permute-done((f32[4,2,128,128]{3,2,0,1:T(8,128)}, f32[4,2,128,128]{3,2,0,1:T(8,128)S(1)}, u32[]{:S(2)}, u32[]{:S(2)}) %collective-permute-start.3) | collective-permute-done | bytes 524320 | tf_op jit(solution)/shard_map/ppermute | solution.py:29
  172.5 5.1 collective-permute-start.4
  178.3 9.8 %collective-permute-done.4 = f32[4,2,128,128]{3,2,0,1:T(8,128)} collective-permute-done((f32[4,2,128,128]{3,2,0,1:T(8,128)}, f32[4,2,128,128]{3,2,0,1:T(8,128)}, u32[]{:S(2)}, u32[]{:S(2)}) %collective-permute-start.4) | collective-permute-done | bytes 524320 | tf_op jit(solution)/shard_map/ppermute | solution.py:29
  212.7 5.6 collective-permute-start.5
  218.9 9.5 %collective-permute-done.5 = f32[4,2,128,128]{3,2,0,1:T(8,128)S(1)} collective-permute-done((f32[4,2,128,128]{3,2,0,1:T(8,128)S(1)}, f32[4,2,128,128]{3,2,0,1:T(8,128)S(1)}, u32[]{:S(2)}, u32[]{:S(2)}) %collective-permute-start.5) | collective-permute-done | bytes 524320 | tf_op jit(solution)/shard_map/ppermute | solution.py:29
  287.2 11.4 %collective-permute-done.6 = f32[4,2,128,128]{3,2,0,1:T(8,128)S(1)} collective-permute-done((f32[4,2,128,128]{3,2,0,1:T(8,128)S(1)}, f32[4,2,128,128]{3,2,0,1:T(8,128)S(1)}, u32[]{:S(2)}, u32[]{:S(2)}) %collective-permute-start.6) | collective-permute-done | bytes 524320 | tf_op jit(solution)/shard_map/ppermute | solution.py:29
  324.9 11.5 %collective-permute-done.7 = f32[4,2,128,128]{3,2,0,1:T(8,128)S(1)} collective-permute-done((f32[4,2,128,128]{3,2,0,1:T(8,128)S(1)}, f32[4,2,128,128]{3,2,0,1:T(8,128)S(1)}, u32[]{:S(2)}, u32[]{:S(2)}) %collective-permute-start.7) | collective-permute-done | bytes 524320 | tf_op jit(solution)/shard_map/ppermute | solution.py:29
  362.8 10.4 %collective-permute-done.8 = f32[4,2,128,128]{3,2,0,1:T(8,128)S(1)} collective-permute-done((f32[4,2,128,128]{3,2,0,1:T(8,128)S(1)}, f32[4,2,128,128]{3,2,0,1:T(8,128)S(1)}, u32[]{:S(2)}, u32[]{:S(2)}) %collective-permute-start.8) | collective-permute-done | bytes 524320 | tf_op jit(solution)/shard_map/ppermute | solution.py:29
  399.4 9.7 %collective-permute-done.9 = f32[4,2,128,128]{3,2,0,1:T(8,128)S(1)} collective-permute-done((f32[4,2,128,128]{3,2,0,1:T(8,128)S(1)}, f32[4,2,128,128]{3,2,0,1:T(8,128)S(1)}, u32[]{:S(2)}, u32[]{:S(2)}) %collective-permute-start.9) | collective-permute-done | bytes 524320 | tf_op jit(solution)/shard_map/ppermute | solution.py:29
  423.4 6.2 %broadcast_in_dim.10 = f32[2,2,384,2048]{3,2,1,0:T(8,128)} broadcast(f32[]{:T(128)} %constant.124.clone.1), dimensions={} | broadcast | bytes 12582916 | tf_op jit(solution)/shard_map/broadcast_in_dim | solution.py:188
  429.6 79.3 %while.16 = (s32[]{:T(128)}, f32[2,2,384,2048]{3,2,1,0:T(8,128)}, s32[8,2]{0,1:T(2,128)S(1)}, f32[8,2,2,128,128]{4,3,0,1,2:T(8,128)S(1)}, s32[]{:T(128)}, /*index=5*/s32[]{:T(128)}, s32[]{:T(128)}, s32[]{:T(128)}) while((s32[]{:T(128)}, f32[2,2,384,2048]{3,2,1,0:T(8,128)}, s32[8,2]{0,1:T(2,128)S(1)}, f32[8,2,2,128,128]{4,3,0,1,2:T(8,128)S(1)}, ...), condition=%wide.region_1.2_spmd, body=%wide.region_0.1_spmd.sunk | while | flops 65544 | bytes 1310933 | solution.py:189
  435.2 4.4 dynamic_update_slice.83
  455.0 4.3 dynamic_update_slice.83
  464.9 4.3 dynamic_update_slice.83
  474.9 4.4 dynamic_update_slice.83
  494.6 4.4 dynamic_update_slice.83
  504.6 4.2 dynamic_update_slice.83
  514.1 4.0 slice.434
  518.1 41.2 %collective-permute-done.10 = f32[2,2,64,2048]{3,2,1,0:T(8,128)S(1)} collective-permute-done((f32[2,2,64,2048]{3,2,1,0:T(8,128)S(1)}, f32[2,2,64,2048]{3,2,1,0:T(8,128)S(1)}, u32[]{:S(2)}, u32[]{:S(2)}) %collective-permute-start.10) | collective-permute-done | bytes 2097184 | tf_op jit(solution)/shard_map/ppermute | solution.py:18
  (480 shorter events, 325.8 us)
Async XLA Ops:
  0.0 6.6 %copy-start.15 = (s32[8,2]{0,1:T(2,128)S(1)}, s32[8,2]{0,1:T(2,128)}, u32[]{:S(2)}) copy-start(s32[8,2]{0,1:T(2,128)} %param.16) | copy-start | bytes 196
  0.0 6.7 %copy-start.1 = (f32[2,128,128]{2,1,0:T(8,128)S(1)}, f32[2,128,128]{2,1,0:T(8,128)}, u32[]{:S(2)}) copy-start(f32[2,128,128]{2,1,0:T(8,128)} %param.13) | copy-start | bytes 393220
  0.0 6.7 %copy-start.14 = (f32[128,128]{1,0:T(8,128)S(1)}, f32[128,128]{1,0:T(8,128)}, u32[]{:S(2)}) copy-start(f32[128,128]{1,0:T(8,128)} %param.14) | copy-start | bytes 196612
  3.2 24.7 %collective-permute-start = (bf16[2,2,64,2048]{3,2,1,0:T(8,128)(2,1)}, bf16[2,2,64,2048]{3,2,1,0:T(8,128)(2,1)S(1)}, u32[]{:S(2)}, u32[]{:S(2)}) collective-permute-start(bf16[2,2,64,2048]{3,2,1,0:T(8,128)(2,1)} %get-tuple-element.143), channel_id=1, source_target_pairs={{0,1},{1,2},{2,3},{3,4},{4,5},{5,6},{6,7},{7,0},{8,9},{9,10},{10,1... | collective-permute-start | bytes 3145736 | tf_op jit(solution)/shard_map/ppermute | solution.py:18
  3.7 25.8 %collective-permute-start.1 = (bf16[2,2,64,2048]{3,2,1,0:T(8,128)(2,1)}, bf16[2,2,64,2048]{3,2,1,0:T(8,128)(2,1)}, u32[]{:S(2)}, u32[]{:S(2)}) collective-permute-start(bf16[2,2,64,2048]{3,2,1,0:T(8,128)(2,1)} %get-tuple-element.144), channel_id=1, source_target_pairs={{1,0},{2,1},{3,2},{4,3},{5,4},{6,5},{7,6},{0,7},{9,8},{10,9},{11,1... | collective-permute-start | bytes 3145736 | tf_op jit(solution)/shard_map/ppermute | solution.py:21
  73.3 4.5 copy-start.4
  87.2 15.0 %collective-permute-start.2 = (f32[4,2,128,128]{3,2,0,1:T(8,128)S(1)}, f32[4,2,128,128]{3,2,0,1:T(8,128)S(1)}, u32[]{:S(2)}, u32[]{:S(2)}) collective-permute-start(f32[4,2,128,128]{3,2,0,1:T(8,128)S(1)} %pad_maximum_fusion.1), channel_id=1, source_target_pairs={{0,8},{8,16},{16,24},{1,9},{9,17},{17,25},{2,10},{10,18},{18,26},{... | collective-permute-start | bytes 1572872 | tf_op jit(solution)/shard_map/ppermute | solution.py:29
  114.3 4.6 copy-start.2
  129.1 16.6 %collective-permute-start.3 = (f32[4,2,128,128]{3,2,0,1:T(8,128)}, f32[4,2,128,128]{3,2,0,1:T(8,128)S(1)}, u32[]{:S(2)}, u32[]{:S(2)}) collective-permute-start(f32[4,2,128,128]{3,2,0,1:T(8,128)} %pad_maximum_fusion.2), channel_id=1, source_target_pairs={{0,8},{8,16},{16,24},{1,9},{9,17},{17,25},{2,10},{10,18},{18,26},{... | collective-permute-start | bytes 1572872 | tf_op jit(solution)/shard_map/ppermute | solution.py:29
  172.5 15.6 %collective-permute-start.4 = (f32[4,2,128,128]{3,2,0,1:T(8,128)}, f32[4,2,128,128]{3,2,0,1:T(8,128)}, u32[]{:S(2)}, u32[]{:S(2)}) collective-permute-start(f32[4,2,128,128]{3,2,0,1:T(8,128)} %pad_maximum_fusion.3), channel_id=1, source_target_pairs={{0,8},{8,16},{16,24},{1,9},{9,17},{17,25},{2,10},{10,18},{18,26},{... | collective-permute-start | bytes 1572872 | tf_op jit(solution)/shard_map/ppermute | solution.py:29
  212.6 5.9 %copy-start.5 = (f32[4,128,128]{2,1,0:T(8,128)S(1)}, f32[4,128,128]{2,1,0:T(8,128)}, u32[]{:S(2)}) copy-start(f32[4,128,128]{2,1,0:T(8,128)} %copy-done.4) | copy-start | bytes 786436
  212.6 5.9 %copy-start.12 = (f32[4,128,128]{2,1,0:T(8,128)S(1)}, f32[4,128,128]{2,1,0:T(8,128)}, u32[]{:S(2)}) copy-start(f32[4,128,128]{2,1,0:T(8,128)} %get-tuple-element.221) | copy-start | bytes 786436
  212.7 15.8 %collective-permute-start.5 = (f32[4,2,128,128]{3,2,0,1:T(8,128)S(1)}, f32[4,2,128,128]{3,2,0,1:T(8,128)S(1)}, u32[]{:S(2)}, u32[]{:S(2)}) collective-permute-start(f32[4,2,128,128]{3,2,0,1:T(8,128)S(1)} %pad_maximum_fusion.4), channel_id=1, source_target_pairs={{0,8},{8,16},{16,24},{1,9},{9,17},{17,25},{2,10},{10,18},{18,26},{... | collective-permute-start | bytes 1572872 | tf_op jit(solution)/shard_map/ppermute | solution.py:29
  245.4 3.4 copy-start.13
  284.1 14.5 %collective-permute-start.6 = (f32[4,2,128,128]{3,2,0,1:T(8,128)S(1)}, f32[4,2,128,128]{3,2,0,1:T(8,128)S(1)}, u32[]{:S(2)}, u32[]{:S(2)}) collective-permute-start(f32[4,2,128,128]{3,2,0,1:T(8,128)S(1)} %pad_maximum_fusion.5), channel_id=1, source_target_pairs={{8,0},{16,8},{24,16},{9,1},{17,9},{25,17},{10,2},{18,10},{26,18},{... | collective-permute-start | bytes 1572872 | tf_op jit(solution)/shard_map/ppermute | solution.py:29
  285.9 1.1 copy-start.7
  320.0 4.5 copy-start.9
  320.8 3.8 copy-start.10
  323.2 13.1 %collective-permute-start.7 = (f32[4,2,128,128]{3,2,0,1:T(8,128)S(1)}, f32[4,2,128,128]{3,2,0,1:T(8,128)S(1)}, u32[]{:S(2)}, u32[]{:S(2)}) collective-permute-start(f32[4,2,128,128]{3,2,0,1:T(8,128)S(1)} %pad_maximum_fusion.6), channel_id=1, source_target_pairs={{8,0},{16,8},{24,16},{9,1},{17,9},{25,17},{10,2},{18,10},{26,18},{... | collective-permute-start | bytes 1572872 | tf_op jit(solution)/shard_map/ppermute | solution.py:29
  360.9 12.3 %collective-permute-start.8 = (f32[4,2,128,128]{3,2,0,1:T(8,128)S(1)}, f32[4,2,128,128]{3,2,0,1:T(8,128)S(1)}, u32[]{:S(2)}, u32[]{:S(2)}) collective-permute-start(f32[4,2,128,128]{3,2,0,1:T(8,128)S(1)} %pad_maximum_fusion.7), channel_id=1, source_target_pairs={{8,0},{16,8},{24,16},{9,1},{17,9},{25,17},{10,2},{18,10},{26,18},{... | collective-permute-start | bytes 1572872 | tf_op jit(solution)/shard_map/ppermute | solution.py:29
  397.7 11.4 %collective-permute-start.9 = (f32[4,2,128,128]{3,2,0,1:T(8,128)S(1)}, f32[4,2,128,128]{3,2,0,1:T(8,128)S(1)}, u32[]{:S(2)}, u32[]{:S(2)}) collective-permute-start(f32[4,2,128,128]{3,2,0,1:T(8,128)S(1)} %pad_maximum_fusion.8), channel_id=1, source_target_pairs={{8,0},{16,8},{24,16},{9,1},{17,9},{25,17},{10,2},{18,10},{26,18},{... | collective-permute-start | bytes 1572872 | tf_op jit(solution)/shard_map/ppermute | solution.py:29
  511.4 47.9 %collective-permute-start.10 = (f32[2,2,64,2048]{3,2,1,0:T(8,128)S(1)}, f32[2,2,64,2048]{3,2,1,0:T(8,128)S(1)}, u32[]{:S(2)}, u32[]{:S(2)}) collective-permute-start(f32[2,2,64,2048]{3,2,1,0:T(8,128)S(1)} %get-tuple-element.142), channel_id=1, source_target_pairs={{0,1},{1,2},{2,3},{3,4},{4,5},{5,6},{6,7},{7,0},{8,9},{9,10},{10,1... | collective-permute-start | bytes 6291464 | tf_op jit(solution)/shard_map/ppermute | solution.py:18
  511.4 49.7 %collective-permute-start.11 = (f32[2,2,64,2048]{3,2,1,0:T(8,128)S(1)}, f32[2,2,64,2048]{3,2,1,0:T(8,128)S(1)}, u32[]{:S(2)}, u32[]{:S(2)}) collective-permute-start(f32[2,2,64,2048]{3,2,1,0:T(8,128)S(1)} %get-tuple-element.141), channel_id=1, source_target_pairs={{1,0},{2,1},{3,2},{4,3},{5,4},{6,5},{7,6},{0,7},{9,8},{10,9},{11,1... | collective-permute-start | bytes 6291464 | tf_op jit(solution)/shard_map/ppermute | solution.py:21
  561.2 3.4 copy-start
  (4 other events, 3.6 us)
where the time goes:
time: 573 us; the launch traced here: 568 us
  matrix products  238 us (42%)
  waiting for transfers between devices  150 us (26%)
  local copies, waits for them, and re-layouts  85.9 us (15%)
  loops' own time  31.4 us (5%)
  starting transfers between devices  30 us (5%)
  other arithmetic  29.2 us (5%)
    ppermute x8, waiting for transfers between devices, passed_along(): return lax.ppermute(array, axis, pairs)  86.1 us
    ppermute x2, waiting for transfers between devices, with_halo(): lax.ppermute(lax.slice_in_dim(block, block.shape[dim] - width, None, axis...  62.2 us
    dynamic_update_slice x8, local copies, waits for them, and re-layouts, add_window(): lax.dynamic_update_slice(total, current + grad_windows[index], (0, 0, cor...  34 us
    dot_general x38, matrix products, transform(): jnp.einsum('bjk,kl->bjl', mid_real, sin_signed, precision=HIGHEST)  33.3 us
    dot_general x38, matrix products, transform(): jnp.einsum('bjk,kl->bjl', mid_imag, sin_signed, precision=HIGHEST)  30.9 us
    another operation x1, loops' own time, body(): grad_strip = lax.fori_loop(0, slots, add_window, grad_strip)  30.8 us
    dot_general x38, matrix products, transform(): jnp.einsum('jk,bkl->bjl', cos_table, wave_imag, precision=HIGHEST)  29.5 us
    dot_general x38, matrix products, transform(): jnp.einsum('jk,bkl->bjl', cos_table, wave_real, precision=HIGHEST)  29.3 us
  transfers between devices with their start and end apart: 12, of which 11 were waited for; matrix products, arithmetic and copies ran while one was open for 2% of the time, Pallas kernels for 0%

commit v1 on v0

v1 whole, which is shorter than its diff:
```python
import functools
import math

import jax
import jax.numpy as jnp
import numpy as np
from jax import lax
from jax.experimental import pallas as pl
from jax.experimental.pallas import tpu as pltpu
from jax.sharding import PartitionSpec as P

DELTA = 0.1
F32, BF16, I32, I16 = jnp.float32, jnp.bfloat16, jnp.int32, jnp.int16
LANES = 128
PACK = 16
STEPS = 32767.0
VMEM = pl.BlockSpec(memory_space=pltpu.VMEM)
SMEM = pl.BlockSpec(memory_space=pltpu.SMEM)
ANY = pl.BlockSpec(memory_space=pl.ANY)


def shifted(array, axis, by):
    count = lax.axis_size(axis)
    return lax.ppermute(array, axis, [(i, (i + by) % count) for i in range(count)])


def matmul(a, b):
    return jnp.dot(a, b, preferred_element_type=F32)


def one_hot(shape, difference):
    rows = lax.broadcasted_iota(I32, shape, 0)
    columns = lax.broadcasted_iota(I32, shape, 1)
    return jnp.where(columns - rows == difference, 1.0, 0.0).astype(BF16)


def column_block(column, columns, width):
    start = jnp.minimum(column // LANES * LANES, columns - width - LANES)
    return pl.multiple_of(start, LANES), column - start


def dft_tables(width):
    index = np.arange(width)
    angle = (index[:, None] * index[None, :] % width) * (2.0 * math.pi / width)
    scale = 1.0 / math.sqrt(width)
    parts = []
    for table in (np.cos(angle) * scale, np.sin(angle) * scale):
        high = table.astype(jnp.bfloat16)
        parts += [high, (table - high.astype(np.float64)).astype(jnp.bfloat16)]
    return np.stack(parts)


def own_kernel(depth, pos, me, source, *refs):
    cleans, others = refs[:depth], refs[depth : 2 * depth]
    held, columns_at, rows_at, sems = refs[2 * depth :]
    per, levels, _, half, width = cleans[0].shape
    tile_rows, columns = source.shape[2:]
    region = width + PACK
    copies = []
    for comp in range(2):
        for level in range(levels):
            copy = pltpu.make_async_copy(
                source.at[comp, level], held.at[comp, level], sems.at[comp, level]
            )
            copy.start()
            copies.append(copy)

    def corner(slot):
        row, column = pos[slot, 0], pos[slot, 1]
        first = jnp.clip((row - half + tile_rows) // PACK * PACK - tile_rows, 0, tile_rows - region)
        return row, pl.multiple_of(first, PACK), column

    for slot in range(depth * per):
        row, first, column = corner(slot)
        _, place = column_block(column, columns, width)
        columns_at[slot] = one_hot((width + LANES, width), -place)
        lead = jnp.where(row >= half, 0, half)
        index = lax.broadcasted_iota(I32, (width, region), 0)
        target = index + jnp.where(index < half, lead, -lead) + row - half - first
        hit = lax.broadcasted_iota(I32, (width, region), 1) == target
        rows_at[slot] = jnp.where(hit, 1.0, 0.0).astype(BF16)
    for comp in range(2):
        for level in range(levels):
            copies[comp * levels + level].wait()
            for by in range(depth):
                for b in range(per):
                    slot = lax.rem(me[0] + by, depth) * per + b
                    row, first, column = corner(slot)
                    start, _ = column_block(column, columns, width)
                    block = held[comp, level, pl.ds(first, region), pl.ds(start, width + LANES)]
                    picked = matmul(block, columns_at[slot]).astype(BF16)
                    picked = matmul(rows_at[slot], picked).astype(BF16)
                    cleans[by][b, level, comp] = picked[:half]
                    others[by][b, level, comp] = picked[half:]


def own_windows(pos, me, transmission, depth, width):
    levels, tile_rows, columns = transmission.shape[1:]
    slots = pos.shape[0]
    per = slots // depth
    piece = jax.ShapeDtypeStruct((per, levels, 2, width // 2, width), BF16)
    return pl.pallas_call(
        functools.partial(own_kernel, depth),
        name="own_windows",
        out_shape=[piece] * (2 * depth),
        in_specs=[SMEM, SMEM, ANY],
        out_specs=[VMEM] * (2 * depth),
        scratch_shapes=[
            pltpu.VMEM(transmission.shape, BF16),
            pltpu.VMEM((slots, width + LANES, width), BF16),
            pltpu.VMEM((slots, width, width + PACK), BF16),
            pltpu.SemaphoreType.DMA((2, levels)),
        ],
    )(pos, me, transmission)


def rim_kernel(pos_prev, pos_next, source, to_prev, to_next, low, high, sems):
    slots, levels, _, half, width = to_prev.shape
    tile_rows, columns = source.shape[2:]
    first = pltpu.make_async_copy(source.at[:, :, pl.ds(0, half), :], low, sems.at[0])
    second = pltpu.make_async_copy(
        source.at[:, :, pl.ds(tile_rows - half, half), :], high, sems.at[1]
    )
    first.start()
    second.start()
    first.wait()
    second.wait()

    def pieces(edge, row, column, out, offset, needed):
        @pl.when(needed)
        def _():
            start, place = column_block(column, columns, width)
            at_columns = one_hot((width + LANES, width), -place)
            at_rows = one_hot((half, half), offset)
            for comp in range(2):
                for level in range(levels):
                    block = edge[comp, level, :, pl.ds(start, width + LANES)]
                    picked = matmul(block, at_columns).astype(BF16)
                    out[level, comp] = matmul(at_rows, picked).astype(BF16)

        @pl.when(jnp.logical_not(needed))
        def _():
            out[...] = jnp.zeros_like(out)

    for slot in range(slots):
        row, column = pos_next[slot, 0], pos_next[slot, 1]
        pieces(high, row, column, to_next.at[slot], row, row < half)
        row, column = pos_prev[slot, 0], pos_prev[slot, 1]
        pieces(low, row, column, to_prev.at[slot], row - tile_rows, row > tile_rows - half)


def rim_pieces(pos_prev, pos_next, transmission, width):
    levels, tile_rows, columns = transmission.shape[1:]
    slots = pos_prev.shape[0]
    piece = jax.ShapeDtypeStruct((slots, levels, 2, width // 2, width), BF16)
    edge = pltpu.VMEM((2, levels, width // 2, columns), BF16)
    return pl.pallas_call(
        rim_kernel,
        name="rim_pieces",
        out_shape=[piece, piece],
        in_specs=[SMEM, SMEM, ANY],
        out_specs=[VMEM, VMEM],
        scratch_shapes=[edge, edge, pltpu.SemaphoreType.DMA((2,))],
    )(pos_prev, pos_next, transmission)


def merge_kernel(depth, pos, me, from_prev, from_next, *refs):
    others, mixed = refs[:depth], refs[depth:]
    per, half = others[0].shape[0], others[0].shape[3]
    for by in range(depth):
        for b in range(per):
            slot = lax.rem(me[0] + by, depth) * per + b
            upper = pos[slot, 0] < half

            @pl.when(upper)
            def _():
                mixed[by][b] = others[by][b] + from_prev[slot]

            @pl.when(jnp.logical_not(upper))
            def _():
                mixed[by][b] = others[by][b] + from_next[slot]


def merged(pos, me, from_prev, from_next, others):
    depth = len(others)
    return pl.pallas_call(
        functools.partial(merge_kernel, depth),
        name="merged",
        out_shape=[jax.ShapeDtypeStruct(o.shape, o.dtype) for o in others],
        in_specs=[SMEM, SMEM] + [VMEM] * (2 + depth),
        out_specs=[VMEM] * depth,
    )(pos, me, from_prev, from_next, *others)


def split(value):
    high = value.astype(BF16)
    return high, (value - high.astype(F32)).astype(BF16)


def build_tables(tables, right, left):
    cos_high, cos_low, sin_high, sin_low = (tables[i] for i in range(4))

    def pair(cos, sin):
        minus = (-sin.astype(F32)).astype(BF16)
        forward = jnp.concatenate(
            [jnp.concatenate([cos, minus], 1), jnp.concatenate([sin, cos], 1)], 0
        )
        inverse = jnp.concatenate(
            [jnp.concatenate([cos, sin], 1), jnp.concatenate([minus, cos], 1)], 0
        )
        return forward, inverse

    one_high, two_high = pair(cos_high, sin_high)
    one_low, two_low = pair(cos_low, sin_low)
    right[0] = jnp.concatenate([one_high, one_high, one_low], 0)
    right[1] = jnp.concatenate([two_high, two_high, two_low], 0)
    left[0] = jnp.concatenate([two_high, two_high, two_low], 1)
    left[1] = jnp.concatenate([one_high, one_high, one_low], 1)


def along_columns(wave, table):
    width = wave[0].shape[0]
    high, low = split(jnp.concatenate(wave, 1))
    out = matmul(jnp.concatenate([high, low, high], 1), table)
    return out[:, :width], out[:, width:]


def along_rows(wave, table):
    width = wave[0].shape[0]
    high, low = split(jnp.concatenate(wave, 0))
    out = matmul(table, jnp.concatenate([high, low, high], 0))
    return out[:width], out[width:]


def times(a, b):
    return a[0] * b[0] - a[1] * b[1], a[0] * b[1] + a[1] * b[0]


def conj_times(a, b):
    return a[0] * b[0] + a[1] * b[1], a[0] * b[1] - a[1] * b[0]


def waves_kernel(depth, pos, me, counts, *refs):
    cleans, mixed = refs[:depth], refs[depth : 2 * depth]
    probe, filt, measured, tables = refs[2 * depth : 2 * depth + 4]
    codes = refs[2 * depth + 4 : 3 * depth + 4]
    window, waves, grads, right, left = refs[3 * depth + 4 :]
    per, levels, _, half, width = cleans[0].shape
    slices = depth * levels
    last = slices - 1
    every = range(per)
    build_tables(tables, right, left)
    for by in range(depth):
        origin = lax.rem(me[0] + depth - by, depth)
        for b in every:
            row = pos[me[0] * per + b, 0]
            lead = pl.multiple_of(jnp.where(row >= half, 0, half), half)
            rest = pl.multiple_of(half - lead, half)
            for level in range(levels):
                for comp in range(2):
                    at = window.at[b, origin * levels + level, comp]
                    at[pl.ds(lead, half), :] = cleans[by][b, level, comp]
                    at[pl.ds(rest, half), :] = mixed[by][b, level, comp]

    def trans(b, s):
        return window[b, s, 0].astype(F32), window[b, s, 1].astype(F32)

    def load(b, s):
        return waves[s, b, 0], waves[s, b, 1]

    def store(b, s, wave):
        waves[s, b, 0] = wave[0]
        waves[s, b, 1] = wave[1]

    def fourier(group):
        group = [along_columns(v, right[0]) for v in group]
        return [along_rows(v, left[0]) for v in group]

    def inverse(group):
        group = [along_rows(v, left[1]) for v in group]
        return [along_columns(v, right[1]) for v in group]

    for b in every:
        store(b, 0, (probe[0], probe[1]))

    def forward(s, carry):
        group = fourier([times(load(b, s), trans(b, s)) for b in every])
        group = inverse([times(v, (filt[0], filt[1])) for v in group])
        for b in every:
            store(b, s + 1, group[b])
        return carry

    lax.fori_loop(0, last, forward, 0)
    far = fourier([times(load(b, last), trans(b, last)) for b in every])
    group = []
    for b in every:
        modulus = jnp.sqrt(far[b][0] * far[b][0] + far[b][1] * far[b][1] + DELTA)
        live = jnp.where(me[0] * per + b < counts[0], 1.0, 0.0).astype(F32)
        weight = live * (modulus - measured[b]) / modulus
        group.append((weight * far[b][0], weight * far[b][1]))
    group = inverse(group)
    for b in every:
        store(b, slices, group[b])

    def emit(b, s, grad):
        piece = conj_times(load(b, s), grad)
        grads[s, b, 0] = piece[0]
        grads[s, b, 1] = piece[1]

    def backward(step, carry):
        s = last - step
        group = [load(b, slices) for b in every]
        for b in every:
            emit(b, s, group[b])
        group = fourier([conj_times(trans(b, s), group[b]) for b in every])
        group = inverse([conj_times((filt[0], filt[1]), v) for v in group])
        for b in every:
            store(b, slices, group[b])
        return carry

    lax.fori_loop(0, last, backward, 0)
    for b in every:
        emit(b, 0, load(b, slices))

    planes = per * levels * 2
    for by in range(depth):
        target = lax.rem(me[0] + by, depth)
        exponents = []
        for b in every:
            for level in range(levels):
                for comp in range(2):
                    value = grads[target * levels + level, b, comp]
                    biggest = jnp.max(jnp.abs(value), axis=0, keepdims=True)
                    power = jnp.floor(jnp.log2(jnp.maximum(biggest, 1e-30))) + 1.0
                    scaled = value * (jnp.exp2(-power) * STEPS)
                    code = jnp.clip(jnp.round(scaled), -STEPS, STEPS)
                    code = code.astype(I32).astype(I16)
                    plane = (b * levels + level) * 2 + comp
                    codes[by][pl.ds(plane * half, half), :] = code[:half]
                    codes[by][pl.ds((planes + plane) * half + planes, half), :] = code[half:]
                    exponents.append(power)
        exponents = jnp.concatenate(exponents, 0).astype(I32).astype(I16)
        codes[by][pl.ds(planes * half, planes), :] = exponents


def window_grads(pos, me, counts, cleans, mixed, probe, filt, measured, tables):
    depth = len(cleans)
    per, levels, _, half, width = cleans[0].shape
    slices = depth * levels
    planes = per * levels * 2
    message = jax.ShapeDtypeStruct((planes * (width + 1), width), I16)
    return pl.pallas_call(
        functools.partial(waves_kernel, depth),
        name="window_grads",
        out_shape=[message] * depth,
        in_specs=[SMEM] * 3 + [VMEM] * (2 * depth + 4),
        out_specs=[VMEM] * depth,
        scratch_shapes=[
            pltpu.VMEM((per, slices, 2, width, width), BF16),
            pltpu.VMEM((slices + 1, per, 2, width, width), F32),
            pltpu.VMEM((slices, per, 2, width, width), F32),
            pltpu.VMEM((2, 6 * width, 2 * width), BF16),
            pltpu.VMEM((2, 2 * width, 6 * width), BF16),
        ],
    )(pos, me, counts, *cleans, *mixed, probe, filt, measured, tables)


def decoded(code, power):
    return code.astype(I32).astype(F32) * (jnp.exp2(power.astype(I32).astype(F32)) * (1.0 / STEPS))


def add_at(total, row, column, value):
    block, place = column // LANES, lax.rem(column, LANES)
    height = value.shape[0]
    value = pltpu.roll(value, place, 1)
    here = lax.broadcasted_iota(I32, value.shape, 1) >= place
    at = total.at[block, pl.ds(row, height), :]
    at[...] += jnp.where(here, value, 0.0)
    at = total.at[block + 1, pl.ds(row, height), :]
    at[...] += jnp.where(here, 0.0, value)


def inner_kernel(depth, levels, pos, me, *refs):
    codes = refs[:depth]
    out, rims, total, sems = refs[depth:]
    width = codes[0].shape[1]
    planes = codes[0].shape[0] // (width + 1)
    half = width // 2
    per = planes // (2 * levels)
    tile_rows = out.shape[2]
    blocks = rims.shape[3]
    copies = []
    for comp in range(2):
        for level in range(levels):
            at = total.at[comp, level]
            at[...] = jnp.zeros(at.shape, F32)
            for by in range(depth):
                for b in range(per):
                    slot = lax.rem(me[0] + depth - by, depth) * per + b
                    plane = (b * levels + level) * 2 + comp
                    power = codes[by][pl.ds(planes * half, planes), :][plane : plane + 1]
                    upper = decoded(codes[by][pl.ds(plane * half, half), :], power)
                    lower = decoded(
                        codes[by][pl.ds((planes + plane) * half + planes, half), :], power
                    )
                    value = jnp.concatenate([upper, lower], 0)
                    add_at(at, pos[slot, 0], pos[slot, 1], value)
            for block in range(blocks):
                copy = pltpu.make_async_copy(
                    at.at[block, pl.ds(width, tile_rows - width), :],
                    out.at[
                        comp, level, pl.ds(half, tile_rows - width), pl.ds(block * LANES, LANES)
                    ],
                    sems.at[comp, level, block],
                )
                copy.start()
                copies.append(copy)
                rims[comp, level, 0, block] = at[block, pl.ds(half, half), :]
                rims[comp, level, 1, block] = at[block, pl.ds(tile_rows, half), :]
    for copy in copies:
        copy.wait()


def inner_sum(pos, me, codes, levels, tile_rows, columns):
    depth = len(codes)
    width = codes[0].shape[1]
    half = width // 2
    blocks = columns // LANES
    return pl.pallas_call(
        functools.partial(inner_kernel, depth, levels),
        name="inner_sum",
        out_shape=[
            jax.ShapeDtypeStruct((2, levels, tile_rows, columns), F32),
            jax.ShapeDtypeStruct((2, levels, 2, blocks, half, LANES), F32),
        ],
        in_specs=[SMEM, SMEM] + [VMEM] * depth,
        out_specs=[ANY, VMEM],
        scratch_shapes=[
            pltpu.VMEM((2, levels, blocks + 1, tile_rows + width, LANES), F32),
            pltpu.SemaphoreType.DMA((2, levels, blocks)),
        ],
    )(pos, me, *codes)


def outer_kernel(depth, pos_prev, pos_next, me, from_prev, from_next, rims, part, out, total, sems):
    _, levels, _, blocks, half, _ = rims.shape
    tile_rows = out.shape[2]
    planes = from_prev.shape[0] // depth // (half + 1)
    per = planes // (2 * levels)
    step = planes * (half + 1)
    copies = []
    for comp in range(2):
        for level in range(levels):
            for side in range(2):
                at = total.at[comp, level, side]
                at[pl.ds(0, blocks), pl.ds(half, half), :] = rims[comp, level, side]
            for by in range(depth):
                for b in range(per):
                    slot = lax.rem(me[0] + depth - by, depth) * per + b
                    plane = (b * levels + level) * 2 + comp
                    row, column = pos_prev[slot, 0], pos_prev[slot, 1]

                    @pl.when(row > tile_rows - half)
                    def _():
                        power = from_prev[pl.ds(by * step, planes), :][plane : plane + 1]
                        code = from_prev[pl.ds(by * step + planes + plane * half, half), :]
                        at = total.at[comp, level, 0]
                        add_at(at, row - tile_rows + half, column, decoded(code, power))

                    row_next, column_next = pos_next[slot, 0], pos_next[slot, 1]

                    @pl.when(row_next < half)
                    def _():
                        power = from_next[pl.ds(by * step + planes * half, planes), :]
                        code = from_next[pl.ds(by * step + plane * half, half), :]
                        at = total.at[comp, level, 1]
                        value = decoded(code, power[plane : plane + 1])
                        add_at(at, row_next + half, column_next, value)

            for side in range(2):
                for block in range(blocks):
                    copy = pltpu.make_async_copy(
                        total.at[comp, level, side, block, pl.ds(half, half), :],
                        out.at[
                            comp,
                            level,
                            pl.ds(side * (tile_rows - half), half),
                            pl.ds(block * LANES, LANES),
                        ],
                        sems.at[comp, level, side, block],
                    )
                    copy.start()
                    copies.append(copy)
    for copy in copies:
        copy.wait()


def outer_sum(pos_prev, pos_next, me, from_prev, from_next, rims, part, depth):
    _, levels, _, blocks, half, _ = rims.shape
    return pl.pallas_call(
        functools.partial(outer_kernel, depth),
        name="outer_sum",
        out_shape=jax.ShapeDtypeStruct(part.shape, F32),
        in_specs=[SMEM] * 3 + [VMEM] * 3 + [ANY],
        out_specs=ANY,
        scratch_shapes=[
            pltpu.VMEM((2, levels, 2, blocks + 1, 3 * half, LANES), F32),
            pltpu.SemaphoreType.DMA((2, levels, 2, blocks)),
        ],
        input_output_aliases={6: 0},
    )(pos_prev, pos_next, me, from_prev, from_next, rims, part)


def body(transmission, probe, propagator, measured, positions, counts):
    width = probe.shape[1]
    half = width // 2
    levels, tile_rows, columns = transmission.shape[1:]
    slots = positions.shape[0]
    depth = lax.axis_size("depth")
    per = slots // depth
    me = lax.axis_index("depth").astype(I32)
    me_ref = me.reshape(1)
    tables = jnp.asarray(dft_tables(width))
    pos_prev = shifted(positions, "tile", 1)
    pos_next = shifted(positions, "tile", -1)
    pieces = own_windows(positions, me_ref, transmission, depth, width)
    cleans, others = pieces[:depth], pieces[depth:]
    cleans = [cleans[0]] + [shifted(cleans[by], "depth", by) for by in range(1, depth)]
    to_prev, to_next = rim_pieces(pos_prev, pos_next, transmission, width)
    from_next = shifted(to_prev, "tile", -1)
    from_prev = shifted(to_next, "tile", 1)
    mixed = merged(positions, me_ref, from_prev, from_next, others)
    mixed = [mixed[0]] + [shifted(mixed[by], "depth", by) for by in range(1, depth)]
    filt = jnp.stack([jnp.cos(propagator), jnp.sin(propagator)])
    mine = lax.dynamic_slice_in_dim(measured, me * per, per, 0)
    codes = window_grads(positions, me_ref, counts, cleans, mixed, probe, filt, mine, tables)
    codes = [codes[0]] + [shifted(codes[by], "depth", by) for by in range(1, depth)]
    planes = per * levels * 2
    upper = jnp.concatenate([c[: planes * (half + 1)] for c in codes], 0)
    lower = jnp.concatenate([c[planes * half :] for c in codes], 0)
    from_next = shifted(upper, "tile", -1)
    from_prev = shifted(lower, "tile", 1)
    part, rims = inner_sum(positions, me_ref, codes, levels, tile_rows, columns)
    return outer_sum(pos_prev, pos_next, me_ref, from_prev, from_next, rims, part, depth)


def solution(mesh):
    in_specs = (
        P(None, "depth", "tile", None),
        P(),
        P(),
        P("tile", None, None),
        P("tile", None),
        P("tile"),
    )
    out_specs = P(None, "depth", "tile", None)
    return jax.shard_map(body, mesh=mesh, in_specs=in_specs, out_specs=out_specs, check_vma=False)
```

time: 573 us -> 117 us (0.20)
  the two profiles are of different devices: /device:TPU:0 before, /device:TPU:11 now
where the time goes in v1:
time: 117 us
  Pallas kernels  48.4 us (41%)
  waiting for transfers between devices  43.2 us (37%)
  starting transfers between devices  16.6 us (14%)
  local copies, waits for them, and re-layouts  5.7 us (5%)
  other arithmetic  1.71 us (1%)
    ppermute x15, waiting for transfers between devices, shifted(): lax.ppermute(array, axis, [(i, (i + by) % count) for i in range(count)])  43.2 us
    pallas_call x1, Pallas kernels, window_grads(): pl.pallas_call(functools.partial(waves_kernel, depth), name='window_grads...  19.2 us
    ppermute x15, starting transfers between devices, shifted(): lax.ppermute(array, axis, [(i, (i + by) % count) for i in range(count)])  16.6 us
    pallas_call x1, Pallas kernels, own_windows(): pl.pallas_call(functools.partial(own_kernel, depth), name='own_windows',...  9.3 us
    pallas_call x1, Pallas kernels, inner_sum(): pl.pallas_call(functools.partial(inner_kernel, depth, levels), name='inne...  6.4 us
    pallas_call x1, Pallas kernels, outer_sum(): pl.pallas_call(functools.partial(outer_kernel, depth), name='outer_sum',...  6.28 us
    pallas_call x1, Pallas kernels, rim_pieces(): pl.pallas_call(rim_kernel, name='rim_pieces', out_shape=[piece, piece], i...  4.71 us
    unnamed x35, local copies, waits for them, and re-layouts  4.41 us
  transfers between devices with their start and end apart: 15, of which 12 were waited for; matrix products, arithmetic and copies ran while one was open for 3% of the time, Pallas kernels for 16%

profile of v1, /device:TPU:11, one launch (start us, length us, event | category | flops | bytes accessed | tf_op | source)
XLA Modules:
  0.0 116.5 jit_solution(10153739229400344493)
XLA Ops:
  1.5 2.0 %collective-permute-start = (s32[8,2]{1,0:T(8,128)S(1)}, s32[8,2]{1,0:T(8,128)S(1)}, u32[]{:S(2)}, u32[]{:S(2)}) collective-permute-start(s32[8,2]{1,0:T(8,128)S(1)} %copy.9.pos), channel_id=1, source_target_pairs={{0,1},{1,2},{2,3},{3,4},{4,5},{5,6},{6,7},{7,0},{8,9},{9,10},{10,1... | collective-permute-start | bytes 200 | tf_op jit(solution)/shard_map/ppermute | solution.py:24
  3.4 1.3 %collective-permute-done.1.pos_next = s32[8,2]{1,0:T(8,128)S(1)} collective-permute-done((s32[8,2]{1,0:T(8,128)S(1)}, s32[8,2]{1,0:T(8,128)S(1)}, u32[]{:S(2)}, u32[]{:S(2)}) %collective-permute-start.1) | collective-permute-done | bytes 96 | tf_op jit(solution)/shard_map/ppermute | solution.py:24
  5.9 4.7 %rim_pieces.1 = (bf16[8,2,2,64,128]{4,3,2,1,0:T(8,128)(2,1)}, bf16[8,2,2,64,128]{4,3,2,1,0:T(8,128)(2,1)}) custom-call(s32[8,2]{1,0:T(8,128)} %copy-done.16, s32[8,2]{1,0:T(8,128)} %copy-done.15, bf16[2,2,256,2048]{3,2,1,0:T(8,128)(2,1)} %source.3), custom_call_target="tpu_custom_call" | custom-call | tf_op jit(solution)/shard_map/rim_pieces/pallas_call | solution.py:157
  10.6 3.3 %collective-permute-start.5 = (bf16[8,2,2,64,128]{4,3,2,1,0:T(8,128)(2,1)}, bf16[8,2,2,64,128]{4,3,2,1,0:T(8,128)(2,1)S(1)}, u32[]{:S(2)}, u32[]{:S(2)}) collective-permute-start(bf16[8,2,2,64,128]{4,3,2,1,0:T(8,128)(2,1)} %get-tuple-element.29), channel_id=1, source_target_pairs={{0,1},{1,2},{2,3},{3,4},{4,5},{5,6},{6,7},{7,0},{8,9},{9,10},{10,1... | collective-permute-start | bytes 1572872 | tf_op jit(solution)/shard_map/ppermute | solution.py:24
  13.9 9.3 %own_windows.1 = (bf16[2,2,2,64,128]{4,3,2,1,0:T(8,128)(2,1)}, bf16[2,2,2,64,128]{4,3,2,1,0:T(8,128)(2,1)}, bf16[2,2,2,64,128]{4,3,2,1,0:T(8,128)(2,1)}, bf16[2,...) custom-call(s32[8,2]{1,0:T(8,128)} %copy-done.13, ...), custom_call_target="tpu_custom_call" | custom-call | tf_op jit(solution)/shard_map/own_windows/pallas_call | solution.py:102
  23.2 1.4 %collective-permute-start.2 = (bf16[2,2,2,64,128]{4,3,2,1,0:T(8,128)(2,1)}, bf16[2,2,2,64,128]{4,3,2,1,0:T(8,128)(2,1)S(1)}, u32[]{:S(2)}, u32[]{:S(2)}) collective-permute-start(bf16[2,2,2,64,128]{4,3,2,1,0:T(8,128)(2,1)} %get-tuple-element.26), channel_id=1, source_target_pairs={{0,8},{8,16},{16,24},{24,0},{1,9},{9,17},{17,25},{25,1},{2,10},{10... | collective-permute-start | bytes 393224 | tf_op jit(solution)/shard_map/ppermute | solution.py:24
  25.6 1.4 %collective-permute-start.4 = (bf16[2,2,2,64,128]{4,3,2,1,0:T(8,128)(2,1)}, bf16[2,2,2,64,128]{4,3,2,1,0:T(8,128)(2,1)S(1)}, u32[]{:S(2)}, u32[]{:S(2)}) collective-permute-start(bf16[2,2,2,64,128]{4,3,2,1,0:T(8,128)(2,1)} %get-tuple-element.28), channel_id=1, source_target_pairs={{0,24},{8,0},{16,8},{24,16},{1,25},{9,1},{17,9},{25,17},{2,26},{10... | collective-permute-start | bytes 393224 | tf_op jit(solution)/shard_map/ppermute | solution.py:24
  28.0 2.4 %merged.1 = (bf16[2,2,2,64,128]{4,3,2,1,0:T(8,128)(2,1)}, bf16[2,2,2,64,128]{4,3,2,1,0:T(8,128)(2,1)}, bf16[2,2,2,64,128]{4,3,2,1,0:T(8,128)(2,1)}, bf16[2,2,2,64,128]{4,3,2,1,0:T(8,128)(2,1)}) custom-call(s32[8,2]{1,0:T(8,128)} %copy-done.13, s32[1]{0:T(128)} %bitcast.me, bf16[8,2,2,64,128]{4,3,2,1,0:T(8,128)(2,1)} %copy-done.5, ...), custom_call_target="tpu_custom_call" | custom-call | tf_op jit(solution)/shard_map/merged/pallas_call | solution.py:186
  30.5 3.1 %collective-permute-start.8 = (bf16[2,2,2,64,128]{4,3,2,1,0:T(8,128)(2,1)}, bf16[2,2,2,64,128]{4,3,2,1,0:T(8,128)(2,1)S(1)}, u32[]{:S(2)}, u32[]{:S(2)}) collective-permute-start(bf16[2,2,2,64,128]{4,3,2,1,0:T(8,128)(2,1)} %get-tuple-element.37), channel_id=1, source_target_pairs={{0,16},{8,24},{16,0},{24,8},{1,17},{9,25},{17,1},{25,9},{2,18},{10... | collective-permute-start | bytes 393224 | tf_op jit(solution)/shard_map/ppermute | solution.py:24
  34.7 1.6 %pad_maximum_fusion = (f32[2,128,128]{2,1,0:T(8,128)}, f32[2,128,128]{2,1,0:T(8,128)}) fusion(f32[1,128,128]{2,1,0:T(8,128)S(1)} %get-tuple-element.54, f32[1,128,128]{2,1,0:T(8,128)S(1)} %get-tuple-element.53, f32[8,128,128]{2,1,0:T(8,128)} %param.10, s32[]{:T(128)S(6)} %select_n.3), kind=kLoop, calls=%fused_computation.2 | loop fusion | flops 32768 | bytes 524292 | tf_op jit(solution)/shard_map/stack | solution.py:534
  36.4 5.9 %collective-permute-done.3.refs_2_ = bf16[2,2,2,64,128]{4,3,2,1,0:T(8,128)(2,1)S(1)} collective-permute-done((bf16[2,2,2,64,128]{4,3,2,1,0:T(8,128)(2,1)}, bf16[2,2,2,64,128]{4,3,2,1,0:T(8,128)(2,1)S(1)}, u32[]{:S(2)}, u32[]{:S(2)}) %collective-permute-start.3) | collective-permute-done | bytes 131104 | tf_op jit(solution)/shard_map/ppermute | solution.py:24
  42.5 2.6 %collective-permute-done.7.refs_5_ = bf16[2,2,2,64,128]{4,3,2,1,0:T(8,128)(2,1)S(1)} collective-permute-done((bf16[2,2,2,64,128]{4,3,2,1,0:T(8,128)(2,1)}, bf16[2,2,2,64,128]{4,3,2,1,0:T(8,128)(2,1)S(1)}, u32[]{:S(2)}, u32[]{:S(2)}) %collective-permute-start.7) | collective-permute-done | bytes 131104 | tf_op jit(solution)/shard_map/ppermute | solution.py:24
  45.1 1.6 %collective-permute-done.8.refs_6_ = bf16[2,2,2,64,128]{4,3,2,1,0:T(8,128)(2,1)S(1)} collective-permute-done((bf16[2,2,2,64,128]{4,3,2,1,0:T(8,128)(2,1)}, bf16[2,2,2,64,128]{4,3,2,1,0:T(8,128)(2,1)S(1)}, u32[]{:S(2)}, u32[]{:S(2)}) %collective-permute-start.8) | collective-permute-done | bytes 131104 | tf_op jit(solution)/shard_map/ppermute | solution.py:24
  46.6 1.5 %collective-permute-done.9.refs_7_ = bf16[2,2,2,64,128]{4,3,2,1,0:T(8,128)(2,1)S(1)} collective-permute-done((bf16[2,2,2,64,128]{4,3,2,1,0:T(8,128)(2,1)}, bf16[2,2,2,64,128]{4,3,2,1,0:T(8,128)(2,1)S(1)}, u32[]{:S(2)}, u32[]{:S(2)}) %collective-permute-start.9) | collective-permute-done | bytes 131104 | tf_op jit(solution)/shard_map/ppermute | solution.py:24
  48.8 19.2 %window_grads.1 = (s16[1032,128]{1,0:T(8,128)(2,1)}, s16[1032,128]{1,0:T(8,128)(2,1)}, s16[1032,128]{1,0:T(8,128)(2,1)}, s16[1032,128]{1,0:T(8,128)(2,1)}) custom-call(s32[8,2]{1,0:T(8,128)} %copy-done.13, s32[1]{0:T(128)} %bitcast.me, s32[1]{0:T(128)S(6)} %copy.16.counts, bf16[2,2,2,64,128]{4,3,2,1,0:T(8,128)(2,1)} %get-tuple-element.25.refs_0_, ...), custom_call_target="tpu_custom_call" | custom-call | tf_op jit(solution)/shard_map/window_grads/pallas_call | solution.py:352
  68.0 1.3 %collective-permute-start.11 = (s16[1032,128]{1,0:T(8,128)(2,1)}, s16[1032,128]{1,0:T(8,128)(2,1)S(1)}, u32[]{:S(2)}, u32[]{:S(2)}) collective-permute-start(s16[1032,128]{1,0:T(8,128)(2,1)} %get-tuple-element.41), channel_id=1, source_target_pairs={{0,16},{8,24},{16,0},{24,8},{1,17},{9,25},{17,1},{25,9},{2,18},{10... | collective-permute-start | bytes 792584 | tf_op jit(solution)/shard_map/ppermute | solution.py:24
  70.4 1.4 %collective-permute-start.12 = (s16[1032,128]{1,0:T(8,128)(2,1)}, s16[1032,128]{1,0:T(8,128)(2,1)S(1)}, u32[]{:S(2)}, u32[]{:S(2)}) collective-permute-start(s16[1032,128]{1,0:T(8,128)(2,1)} %get-tuple-element.42), channel_id=1, source_target_pairs={{0,24},{8,0},{16,8},{24,16},{1,25},{9,1},{17,9},{25,17},{2,26},{10... | collective-permute-start | bytes 792584 | tf_op jit(solution)/shard_map/ppermute | solution.py:24
  71.8 3.9 %collective-permute-done.10.refs_1_ = s16[1032,128]{1,0:T(8,128)(2,1)S(1)} collective-permute-done((s16[1032,128]{1,0:T(8,128)(2,1)}, s16[1032,128]{1,0:T(8,128)(2,1)S(1)}, u32[]{:S(2)}, u32[]{:S(2)}) %collective-permute-start.10) | collective-permute-done | bytes 264224 | tf_op jit(solution)/shard_map/ppermute | solution.py:24
  75.8 15.1 %collective-permute-done.11.refs_2_ = s16[1032,128]{1,0:T(8,128)(2,1)S(1)} collective-permute-done((s16[1032,128]{1,0:T(8,128)(2,1)}, s16[1032,128]{1,0:T(8,128)(2,1)S(1)}, u32[]{:S(2)}, u32[]{:S(2)}) %collective-permute-start.11) | collective-permute-done | bytes 264224 | tf_op jit(solution)/shard_map/ppermute | solution.py:24
  90.9 2.4 %collective-permute-done.12.refs_3_ = s16[1032,128]{1,0:T(8,128)(2,1)S(1)} collective-permute-done((s16[1032,128]{1,0:T(8,128)(2,1)}, s16[1032,128]{1,0:T(8,128)(2,1)S(1)}, u32[]{:S(2)}, u32[]{:S(2)}) %collective-permute-start.12) | collective-permute-done | bytes 264224 | tf_op jit(solution)/shard_map/ppermute | solution.py:24
  94.4 6.4 %inner_sum.1 = (f32[2,2,256,2048]{3,2,1,0:T(8,128)}, f32[2,2,2,16,64,128]{5,4,3,2,1,0:T(8,128)}) custom-call(s32[8,2]{1,0:T(8,128)} %copy-done.13, s32[1]{0:T(128)} %bitcast.me, s16[1032,128]{1,0:T(8,128)(2,1)} %get-tuple-element.39.refs_0_, s16[1032,128]{1,0:T(8,128)(2,1)} %copy-done, s16[1032,128]{1,0:T(8,128)(2,1)} %copy-done.1, s16[1032,128]{1,0:T(8,128)(2,1)} %copy-done.2), custom_call_target="tpu_custom_call" | custom-call | tf_op jit(solution)/shard_map/inner_sum/pallas_call | solution.py:429
  100.9 3.2 %collective-permute-done.13.from_prev = s16[2080,128]{1,0:T(8,128)(2,1)S(1)} collective-permute-done((s16[2080,128]{1,0:T(8,128)(2,1)S(1)}, s16[2080,128]{1,0:T(8,128)(2,1)S(1)}, u32[]{:S(2)}, u32[]{:S(2)}) %collective-permute-start.13) | collective-permute-done | bytes 532512 | tf_op jit(solution)/shard_map/ppermute | solution.py:24
  104.0 5.2 %collective-permute-done.14.from_next = s16[2080,128]{1,0:T(8,128)(2,1)S(1)} collective-permute-done((s16[2080,128]{1,0:T(8,128)(2,1)S(1)}, s16[2080,128]{1,0:T(8,128)(2,1)S(1)}, u32[]{:S(2)}, u32[]{:S(2)}) %collective-permute-start.14) | collective-permute-done | bytes 532512 | tf_op jit(solution)/shard_map/ppermute | solution.py:24
  110.1 6.3 %outer_sum.1 = f32[2,2,256,2048]{3,2,1,0:T(8,128)} custom-call(s32[8,2]{1,0:T(8,128)} %copy-done.16, s32[8,2]{1,0:T(8,128)} %copy-done.15, s32[1]{0:T(128)} %bitcast.me, s16[2080,128]{1,0:T(8,128)(2,1)} %copy-done.3, s16[2080,128]{1,0:T(8,128)(2,1)} %copy-done.4, f32[2,2,2,16,64,128]{5,4,3,2,1,0:T(8,128)} %get-tuple-element.43.rims, ...), custom_call_target="tpu_custom_call", output_to_operand_aliasing={{}: (6, {})} | custom-call | tf_op jit(solution)/shard_map/outer_sum/pallas_call | solution.py:500
  (55 shorter events, 9.1 us)
Async XLA Ops:
  0.0 33.8 %copy-start.14 = (f32[128,128]{1,0:T(8,128)S(1)}, f32[128,128]{1,0:T(8,128)}, u32[]{:S(2)}) copy-start(f32[128,128]{1,0:T(8,128)} %param.9) | copy-start | bytes 196612
  0.8 13.1 %copy-start.13 = (s32[8,2]{1,0:T(8,128)}, s32[8,2]{1,0:T(8,128)S(1)}, u32[]{:S(2)}) copy-start(s32[8,2]{1,0:T(8,128)S(1)} %copy.9.pos) | copy-start | bytes 196
  0.8 3.9 %collective-permute-start.1 = (s32[8,2]{1,0:T(8,128)S(1)}, s32[8,2]{1,0:T(8,128)S(1)}, u32[]{:S(2)}, u32[]{:S(2)}) collective-permute-start(s32[8,2]{1,0:T(8,128)S(1)} %copy.9.pos), channel_id=1, source_target_pairs={{0,7},{1,0},{2,1},{3,2},{4,3},{5,4},{6,5},{7,6},{8,15},{9,8},{10,9... | collective-permute-start | bytes 200 | tf_op jit(solution)/shard_map/ppermute | solution.py:24
  1.5 3.3 %collective-permute-start = (s32[8,2]{1,0:T(8,128)S(1)}, s32[8,2]{1,0:T(8,128)S(1)}, u32[]{:S(2)}, u32[]{:S(2)}) collective-permute-start(s32[8,2]{1,0:T(8,128)S(1)} %copy.9.pos), channel_id=1, source_target_pairs={{0,1},{1,2},{2,3},{3,4},{4,5},{5,6},{6,7},{7,0},{8,9},{9,10},{10,1... | collective-permute-start | bytes 200 | tf_op jit(solution)/shard_map/ppermute | solution.py:24
  10.6 16.4 %collective-permute-start.5 = (bf16[8,2,2,64,128]{4,3,2,1,0:T(8,128)(2,1)}, bf16[8,2,2,64,128]{4,3,2,1,0:T(8,128)(2,1)S(1)}, u32[]{:S(2)}, u32[]{:S(2)}) collective-permute-start(bf16[8,2,2,64,128]{4,3,2,1,0:T(8,128)(2,1)} %get-tuple-element.29), channel_id=1, source_target_pairs={{0,1},{1,2},{2,3},{3,4},{4,5},{5,6},{6,7},{7,0},{8,9},{9,10},{10,1... | collective-permute-start | bytes 1572872 | tf_op jit(solution)/shard_map/ppermute | solution.py:24
  13.9 13.2 %collective-permute-start.6 = (bf16[8,2,2,64,128]{4,3,2,1,0:T(8,128)(2,1)}, bf16[8,2,2,64,128]{4,3,2,1,0:T(8,128)(2,1)S(1)}, u32[]{:S(2)}, u32[]{:S(2)}) collective-permute-start(bf16[8,2,2,64,128]{4,3,2,1,0:T(8,128)(2,1)} %get-tuple-element.30), channel_id=1, source_target_pairs={{0,7},{1,0},{2,1},{3,2},{4,3},{5,4},{6,5},{7,6},{8,15},{9,8},{10,9... | collective-permute-start | bytes 1572872 | tf_op jit(solution)/shard_map/ppermute | solution.py:24
  23.2 10.6 %collective-permute-start.2 = (bf16[2,2,2,64,128]{4,3,2,1,0:T(8,128)(2,1)}, bf16[2,2,2,64,128]{4,3,2,1,0:T(8,128)(2,1)S(1)}, u32[]{:S(2)}, u32[]{:S(2)}) collective-permute-start(bf16[2,2,2,64,128]{4,3,2,1,0:T(8,128)(2,1)} %get-tuple-element.26), channel_id=1, source_target_pairs={{0,8},{8,16},{16,24},{24,0},{1,9},{9,17},{17,25},{25,1},{2,10},{10... | collective-permute-start | bytes 393224 | tf_op jit(solution)/shard_map/ppermute | solution.py:24
  24.5 17.7 %collective-permute-start.3 = (bf16[2,2,2,64,128]{4,3,2,1,0:T(8,128)(2,1)}, bf16[2,2,2,64,128]{4,3,2,1,0:T(8,128)(2,1)S(1)}, u32[]{:S(2)}, u32[]{:S(2)}) collective-permute-start(bf16[2,2,2,64,128]{4,3,2,1,0:T(8,128)(2,1)} %get-tuple-element.27), channel_id=1, source_target_pairs={{0,16},{8,24},{16,0},{24,8},{1,17},{9,25},{17,1},{25,9},{2,18},{10... | collective-permute-start | bytes 393224 | tf_op jit(solution)/shard_map/ppermute | solution.py:24
  25.6 16.9 %collective-permute-start.4 = (bf16[2,2,2,64,128]{4,3,2,1,0:T(8,128)(2,1)}, bf16[2,2,2,64,128]{4,3,2,1,0:T(8,128)(2,1)S(1)}, u32[]{:S(2)}, u32[]{:S(2)}) collective-permute-start(bf16[2,2,2,64,128]{4,3,2,1,0:T(8,128)(2,1)} %get-tuple-element.28), channel_id=1, source_target_pairs={{0,24},{8,0},{16,8},{24,16},{1,25},{9,1},{17,9},{25,17},{2,26},{10... | collective-permute-start | bytes 393224 | tf_op jit(solution)/shard_map/ppermute | solution.py:24
  30.4 14.7 %collective-permute-start.7 = (bf16[2,2,2,64,128]{4,3,2,1,0:T(8,128)(2,1)}, bf16[2,2,2,64,128]{4,3,2,1,0:T(8,128)(2,1)S(1)}, u32[]{:S(2)}, u32[]{:S(2)}) collective-permute-start(bf16[2,2,2,64,128]{4,3,2,1,0:T(8,128)(2,1)} %get-tuple-element.36), channel_id=1, source_target_pairs={{0,8},{8,16},{16,24},{24,0},{1,9},{9,17},{17,25},{25,1},{2,10},{10... | collective-permute-start | bytes 393224 | tf_op jit(solution)/shard_map/ppermute | solution.py:24
  30.5 16.2 %collective-permute-start.8 = (bf16[2,2,2,64,128]{4,3,2,1,0:T(8,128)(2,1)}, bf16[2,2,2,64,128]{4,3,2,1,0:T(8,128)(2,1)S(1)}, u32[]{:S(2)}, u32[]{:S(2)}) collective-permute-start(bf16[2,2,2,64,128]{4,3,2,1,0:T(8,128)(2,1)} %get-tuple-element.37), channel_id=1, source_target_pairs={{0,16},{8,24},{16,0},{24,8},{1,17},{9,25},{17,1},{25,9},{2,18},{10... | collective-permute-start | bytes 393224 | tf_op jit(solution)/shard_map/ppermute | solution.py:24
  33.8 14.3 %copy-start.7 = (bf16[2,2,2,64,128]{4,3,2,1,0:T(8,128)(2,1)}, bf16[2,2,2,64,128]{4,3,2,1,0:T(8,128)(2,1)S(1)}, u32[]{:S(2)}) copy-start(bf16[2,2,2,64,128]{4,3,2,1,0:T(8,128)(2,1)S(1)} %collective-permute-done.2.refs_1_) | copy-start | bytes 393220
  33.8 14.3 %collective-permute-start.9 = (bf16[2,2,2,64,128]{4,3,2,1,0:T(8,128)(2,1)}, bf16[2,2,2,64,128]{4,3,2,1,0:T(8,128)(2,1)S(1)}, u32[]{:S(2)}, u32[]{:S(2)}) collective-permute-start(bf16[2,2,2,64,128]{4,3,2,1,0:T(8,128)(2,1)} %get-tuple-element.38), channel_id=1, source_target_pairs={{0,24},{8,0},{16,8},{24,16},{1,25},{9,1},{17,9},{25,17},{2,26},{10... | collective-permute-start | bytes 393224 | tf_op jit(solution)/shard_map/ppermute | solution.py:24
  42.3 5.9 %copy-start.8 = (bf16[2,2,2,64,128]{4,3,2,1,0:T(8,128)(2,1)}, bf16[2,2,2,64,128]{4,3,2,1,0:T(8,128)(2,1)S(1)}, u32[]{:S(2)}) copy-start(bf16[2,2,2,64,128]{4,3,2,1,0:T(8,128)(2,1)S(1)} %collective-permute-done.3.refs_2_) | copy-start | bytes 393220
  42.5 5.6 %copy-start.9 = (bf16[2,2,2,64,128]{4,3,2,1,0:T(8,128)(2,1)}, bf16[2,2,2,64,128]{4,3,2,1,0:T(8,128)(2,1)S(1)}, u32[]{:S(2)}) copy-start(bf16[2,2,2,64,128]{4,3,2,1,0:T(8,128)(2,1)S(1)} %collective-permute-done.4.refs_3_) | copy-start | bytes 393220
  45.1 3.1 %copy-start.10 = (bf16[2,2,2,64,128]{4,3,2,1,0:T(8,128)(2,1)}, bf16[2,2,2,64,128]{4,3,2,1,0:T(8,128)(2,1)S(1)}, u32[]{:S(2)}) copy-start(bf16[2,2,2,64,128]{4,3,2,1,0:T(8,128)(2,1)S(1)} %collective-permute-done.7.refs_5_) | copy-start | bytes 393220
  68.0 7.7 %collective-permute-start.10 = (s16[1032,128]{1,0:T(8,128)(2,1)}, s16[1032,128]{1,0:T(8,128)(2,1)S(1)}, u32[]{:S(2)}, u32[]{:S(2)}) collective-permute-start(s16[1032,128]{1,0:T(8,128)(2,1)} %get-tuple-element.40), channel_id=1, source_target_pairs={{0,8},{8,16},{16,24},{24,0},{1,9},{9,17},{17,25},{25,1},{2,10},{10... | collective-permute-start | bytes 792584 | tf_op jit(solution)/shard_map/ppermute | solution.py:24
  68.0 22.9 %collective-permute-start.11 = (s16[1032,128]{1,0:T(8,128)(2,1)}, s16[1032,128]{1,0:T(8,128)(2,1)S(1)}, u32[]{:S(2)}, u32[]{:S(2)}) collective-permute-start(s16[1032,128]{1,0:T(8,128)(2,1)} %get-tuple-element.41), channel_id=1, source_target_pairs={{0,16},{8,24},{16,0},{24,8},{1,17},{9,25},{17,1},{25,9},{2,18},{10... | collective-permute-start | bytes 792584 | tf_op jit(solution)/shard_map/ppermute | solution.py:24
  70.4 23.0 %collective-permute-start.12 = (s16[1032,128]{1,0:T(8,128)(2,1)}, s16[1032,128]{1,0:T(8,128)(2,1)S(1)}, u32[]{:S(2)}, u32[]{:S(2)}) collective-permute-start(s16[1032,128]{1,0:T(8,128)(2,1)} %get-tuple-element.42), channel_id=1, source_target_pairs={{0,24},{8,0},{16,8},{24,16},{1,25},{9,1},{17,9},{25,17},{2,26},{10... | collective-permute-start | bytes 792584 | tf_op jit(solution)/shard_map/ppermute | solution.py:24
  75.7 18.7 %copy-start = (s16[1032,128]{1,0:T(8,128)(2,1)}, s16[1032,128]{1,0:T(8,128)(2,1)S(1)}, u32[]{:S(2)}) copy-start(s16[1032,128]{1,0:T(8,128)(2,1)S(1)} %collective-permute-done.10.refs_1_) | copy-start | bytes 792580
  90.9 3.5 %copy-start.1 = (s16[1032,128]{1,0:T(8,128)(2,1)}, s16[1032,128]{1,0:T(8,128)(2,1)S(1)}, u32[]{:S(2)}) copy-start(s16[1032,128]{1,0:T(8,128)(2,1)S(1)} %collective-permute-done.11.refs_2_) | copy-start | bytes 792580
  93.4 10.6 %collective-permute-start.13 = (s16[2080,128]{1,0:T(8,128)(2,1)S(1)}, s16[2080,128]{1,0:T(8,128)(2,1)S(1)}, u32[]{:S(2)}, u32[]{:S(2)}) collective-permute-start(s16[2080,128]{1,0:T(8,128)(2,1)S(1)} %pad_add_fusion), channel_id=1, source_target_pairs={{0,1},{1,2},{2,3},{3,4},{4,5},{5,6},{6,7},{7,0},{8,9},{9,10},{10,1... | collective-permute-start | bytes 1597448 | tf_op jit(solution)/shard_map/ppermute | solution.py:24
  94.2 15.1 %collective-permute-start.14 = (s16[2080,128]{1,0:T(8,128)(2,1)S(1)}, s16[2080,128]{1,0:T(8,128)(2,1)S(1)}, u32[]{:S(2)}, u32[]{:S(2)}) collective-permute-start(s16[2080,128]{1,0:T(8,128)(2,1)S(1)} %pad_add_fusion.1), channel_id=1, source_target_pairs={{0,7},{1,0},{2,1},{3,2},{4,3},{5,4},{6,5},{7,6},{8,15},{9,8},{10,9... | collective-permute-start | bytes 1597448 | tf_op jit(solution)/shard_map/ppermute | solution.py:24
  104.0 5.3 %copy-start.3 = (s16[2080,128]{1,0:T(8,128)(2,1)}, s16[2080,128]{1,0:T(8,128)(2,1)S(1)}, u32[]{:S(2)}) copy-start(s16[2080,128]{1,0:T(8,128)(2,1)S(1)} %collective-permute-done.13.from_prev) | copy-start | bytes 1597444
  (8 other events, 7.0 us)
